TPU v7x, 32 devices: a whole 2x2x4 slice. The times are simulated.
32 devices in a mesh: row: 4 (over x, core), grp: 8 (over z, y).
Axes of the slice: x: 2, y: 2, z: 4, core: 2. Of those that a mesh axis runs over, the one named last changes fastest.
Arguments:
- integrals: bfloat16 [32, 512, 256], P('grp', 'row'), may hold values from -1.1953125 to 1.1953125
- amplitudes: bfloat16 [32, 1024, 256], P('grp', 'row'), may hold values from -1.796875 to 1.796875
- pair_orbs: int32 [32, 8], P('grp', 'row'), may hold values from 0 to 3, as said below
- pair_count: int32 [8, 4], P('grp', 'row'), may hold values from 1 to 4, as said below
- neighbours: int32 [32, 16], P('grp', 'row'), may hold values from 0 to 11
- coupling: float32 [32, 16], P('grp', 'row'), may hold values from -1.8 to 1.8
- bases: bfloat16 [32, 1024, 256], P('grp', 'row'), may hold values from -0.375 to 0.375
- virt_energy: float32 [32, 1024], P('grp', 'row'), may hold values from 0.3 to 3
- occ_energy: float32 [32, 4], P('grp', 'row'), may hold values from -1.5 to -0.3
Outputs:
- residual: float32 [32, 1024, 256], P('grp', 'row')
Inputs may be any that keep to these rules, and one draw needn't show every extreme that they name: `pair_orbs`: in the columns of row r the first orbital of every pair is orbital r of the group, the one owned by that device; the second is any orbital of the group. `pair_count`: live slots come first on each device; some device holds 4 live pairs in every draw.
All inputs are finite; a program needn't handle non-finite values.
Results may differ from a plain program's by a relative error of at most 0.0007.
Values may be sent and summed in bfloat16 or wider, within the bound.
No kernel may reach another device: no remote copies, remote signals or barrier semaphores. Data moves between devices by JAX's collectives and lax.ppermute only.
A program may use at most 64 MiB of HBM per device.

v0:
```python
import functools

import jax
import jax.numpy as jnp
from jax import lax
from jax.experimental import pallas as pl
from jax.experimental.pallas import tpu as pltpu
from jax.sharding import PartitionSpec as P


BF16 = jnp.bfloat16
F32 = jnp.float32
VMEM = pltpu.VMEM
SMEM = pltpu.SMEM
HBM = pltpu.HBM
GRANT = 8 << 20


def dot(a, b, dims):
    return lax.dot_general(a, b, (dims, ((), ())), preferred_element_type=F32)


def call(kernel, outs, inputs, flops, scratch=(), aliases=()):
    values, specs = [], []
    for space, value in inputs:
        if space in (VMEM, HBM):
            value = pltpu.with_memory_space_constraint(value, space)
        values.append(value)
        specs.append(pl.BlockSpec(memory_space=space))
    shapes, out_specs = [], []
    for space, shape, dtype in outs:
        plain = space is pl.ANY
        shapes.append(jax.ShapeDtypeStruct(shape, dtype) if plain else space(shape, dtype))
        out_specs.append(pl.BlockSpec(memory_space=space))
    size = sum(value.size * value.dtype.itemsize for value in values)
    return pl.pallas_call(
        kernel,
        out_shape=shapes,
        in_specs=specs,
        out_specs=out_specs,
        scratch_shapes=scratch,
        input_output_aliases=dict(aliases),
        cost_estimate=pl.CostEstimate(flops=flops, bytes_accessed=16 * size, transcendentals=0),
        compiler_params=pltpu.CompilerParams(vmem_limit_bytes=GRANT),
    )(*values)


def transform(base, amp):
    first = dot(base, amp, ((1,), (0,))).astype(BF16)
    return dot(first, base, ((1,), (1,))).astype(BF16)


def lead_kernel(amps, bases, *refs):
    small = (len(refs) - 4) // 2
    sources, (out, amps_out, bases_out) = refs[:small], refs[small : small + 3]
    targets, sems = refs[small + 3 : -1], refs[-1]
    width = amps.shape[0]
    loads = [
        [
            pltpu.make_async_copy(bases.at[slot], bases_out.at[slot], sems.at[0, slot]),
            pltpu.make_async_copy(amps.at[slot], amps_out.at[slot], sems.at[1, slot]),
        ]
        for slot in range(width)
    ]
    others = [
        pltpu.make_async_copy(source, target, sems.at[2, n])
        for n, (source, target) in enumerate(zip(sources, targets))
    ]
    for load in sum(loads, []) + others:
        load.start()
    for load in loads[0]:
        load.wait()
    out[...] = transform(bases_out[0], amps_out[0])
    for load in sum(loads[1:], []) + others:
        load.wait()


def rest_kernel(count, amps, bases, *outs):
    for slot, out in enumerate(outs, 1):
        amp = jnp.where(slot < count[0, 0], amps[slot], jnp.zeros((), BF16))
        out[...] = transform(bases[slot], amp)


def mark_kernel(source, out):
    out[...] = source[...]


def in_halves(count, width, work):
    half = width // 2
    work(range(half))

    @pl.when(count[0, 0] > half)
    def _():
        work(range(half, width))


def integ_kernel(orbs, occ, count, energy, amps, *refs):
    pieces, (out, held, sems) = refs[:-3], refs[-3:]
    width = amps.shape[0]
    loads = [pltpu.make_async_copy(amps.at[s], held.at[s], sems.at[s]) for s in range(width)]
    for load in loads:
        load.start()
    column = energy[...].T
    left = [piece[orbs[0, 0]].T for piece in pieces]

    def products(slots):
        for slot in slots:
            terms = [dot(a, b[orbs[1, slot]], ((1,), (0,))) for a, b in zip(left, pieces)]
            out[slot] = sum(terms[1:], terms[0])

    def energies(slots):
        for slot in slots:
            denom = column[:, slot : slot + 1] + energy[slot : slot + 1, :] - occ[0, slot]
            out[slot] += denom * held[slot].astype(F32)

    in_halves(count, width, products)
    for load in loads:
        load.wait()
    in_halves(count, width, energies)


def add_tiles(rows, columns, weights, tiles, out, slots, before):
    total = weights.shape[0] // out.shape[0]

    def step(block, carry):
        at = pl.ds(pl.multiple_of(block * rows, rows), rows)
        values = [tile[at, :].astype(F32) for tile in tiles]
        for slot in slots:
            acc = out[slot, at, :] if before else None
            for m, value in zip(columns, values):
                row = slot * total + m
                term = weights[row : row + 1, :] * value
                acc = term if acc is None else acc + term
            out[slot, at, :] = acc
        return carry

    lax.fori_loop(0, out.shape[1] // rows, step, 0)


def gather_kernel(columns, count, weights, *refs):
    tiles, (out, held, sems) = refs[:-3], refs[-3:]
    width = out.shape[0]
    own, tiles = tiles[:width], tiles[width:]
    loads = [pltpu.make_async_copy(own[s], held.at[s], sems.at[s]) for s in range(width)]
    for load in loads:
        load.start()
    in_halves(count, width, lambda slots: add_tiles(16, columns, weights, tiles, out, slots, False))
    for load in loads:
        load.wait()
    own = [held.at[s] for s in range(width)]
    place = range(width, 2 * width)
    in_halves(count, width, lambda slots: add_tiles(16, place, weights, own, out, slots, True))


def final_kernel(columns, count, token, weights, base, bases, sums, *refs):
    tiles, (out, held, sems) = refs[:-3], refs[-3:]
    width = base.shape[0]
    half = width // 2
    total = weights.shape[0] // width
    stores = [pltpu.make_async_copy(held.at[s], out.at[s], sems.at[s]) for s in range(width)]

    @pl.when(count[0, 0] <= half)
    def _():
        for slot in range(half, width):
            held[slot] = jnp.zeros(held.shape[1:], F32)
            stores[slot].start()

    def some(slots):
        combined = []
        for slot in slots:
            acc = sums[slot]
            for m, tile in zip(columns, tiles):
                row = slot * total + m
                acc = acc + weights[row : row + 1, :] * tile[...].astype(F32)
            combined.append(acc.astype(BF16))
        firsts = [dot(bases[s], c, ((0,), (0,))).astype(BF16) for s, c in zip(slots, combined)]
        for slot, first in zip(slots, firsts):
            back = dot(first, bases[slot], ((1,), (0,)))
            value = base[slot] - back
            held[slot] = jnp.where(slot < count[0, 0], value, jnp.float32(0))
            stores[slot].start()

    in_halves(count, width, some)
    for store in stores:
        store.wait()


def row_pieces(array):
    count = lax.axis_size("row")
    pieces = [array]
    if count & (count - 1):
        for shift in range(1, count):
            pairs = [(i, (i + shift) % count) for i in range(count)]
            pieces.append(lax.ppermute(array, "row", pairs))
        return pieces
    step = count // 2
    while step:
        pairs = [(i, i ^ step) for i in range(count)]
        piece = jnp.concatenate(pieces, axis=1)
        pieces = [piece, lax.ppermute(piece, "row", pairs)]
        step //= 2
    return pieces


def tile_weights(neighbours, coupling, width, virt):
    levels = lax.axis_size("grp") // 2
    group = lax.axis_index("grp")
    level = lax.shift_right_logical(group, 1)
    even = (group & 1) == 0
    inside = jnp.where(even, level > 0, level < levels - 1)
    block = (neighbours >= width).astype(jnp.int32) + (neighbours >= 2 * width).astype(jnp.int32)
    kind = jnp.where(even, 2 - block, block)
    scale = jnp.where((kind < 2) | inside, coupling, 0.0)
    place = neighbours + (kind - block) * width
    shape = (width, 3 * width, virt, neighbours.shape[1])
    index = lax.broadcasted_iota(jnp.int32, shape, 1)
    hit = place[:, None, None, :] == index
    table = jnp.sum(jnp.where(hit, scale[:, None, None, :], 0.0), axis=3)
    return table.reshape(width * 3 * width, virt)


def local(
    integrals,
    amplitudes,
    pair_orbs,
    pair_count,
    neighbours,
    coupling,
    bases,
    virt_energy,
    occ_energy,
):
    width, virt = amplitudes.shape[0], amplitudes.shape[1]
    count = lax.axis_size("grp")
    cube = 2 * virt * virt * virt
    tile = (VMEM, (virt, virt), BF16)
    stack = (VMEM, (width, virt, virt), BF16)
    wide = (VMEM, (width, virt, virt), F32)
    last = width - 1
    dma = pltpu.SemaphoreType.DMA

    small = (neighbours, coupling, virt_energy, pair_orbs.T, occ_energy.T)
    own, amps, basis, *small = call(
        lead_kernel,
        [tile, stack, stack] + [(VMEM, value.shape, value.dtype) for value in small],
        [(HBM, amplitudes), (HBM, bases)] + [(HBM, value) for value in small],
        2 * cube, [dma((3, max(width, len(small))))],
    )
    neighbours, coupling, virt_energy, orbs, occ = small
    own = [own] + list(call(
        rest_kernel, [tile] * last, [(SMEM, pair_count), (VMEM, amps), (VMEM, basis)],
        2 * last * cube,
    ))
    weights = tile_weights(neighbours, coupling, width, virt)

    swap = [(i, i ^ 1) for i in range(count)]
    ring = [(i, (i + 2) % count if i % 2 == 0 else (i - 2) % count) for i in range(count)]
    path = list(range(0, count, 2)) + list(range(count - 1, 0, -2))
    cycle = list(zip(path, path[1:] + path[:1]))
    half = width // 2
    near = [lax.ppermute(t, "grp", swap) for t in own]
    far = [lax.ppermute(t, "grp", ring if n in (0, 2) else cycle) for n, t in enumerate(near)]
    token = neighbours
    for _ in range(width):
        mark = [(VMEM, token.shape, token.dtype)]
        token = call(mark_kernel, mark, [(VMEM, token)], 1)[0]

    pieces = row_pieces(integrals)
    aux = sum(piece.shape[1] for piece in pieces)
    base = call(
        integ_kernel, [wide],
        [(SMEM, orbs), (SMEM, occ), (SMEM, pair_count), (VMEM, virt_energy), (HBM, amplitudes)]
        + [(VMEM, piece) for piece in pieces], 2 * width * virt * virt * aux,
        [VMEM((width, virt, virt), BF16), dma((width,))],
    )[0]
    place = list(range(width)) + list(range(2 * width, 2 * width + half))
    sums = call(
        functools.partial(gather_kernel, place), [wide],
        [(SMEM, pair_count), (VMEM, weights)] + [(HBM, t) for t in own]
        + [(VMEM, t) for t in near + far[:half]],
        8 * width * virt * virt, [VMEM((width, virt, virt), BF16), dma((width,))],
    )[0]
    return call(
        functools.partial(final_kernel, range(2 * width + half, 3 * width)),
        [(pl.ANY, (width, virt, virt), F32)],
        [(SMEM, pair_count), (VMEM, token), (VMEM, weights), (VMEM, base), (VMEM, bases), (VMEM, sums)]
        + [(VMEM, t) for t in far[half:]],
        2 * width * cube, [VMEM((width, virt, virt), F32), dma((width,))],
    )[0]


def solution(mesh):
    placed = (
        P("grp", "row", None),
        P("grp", "row", None),
        P("grp", "row"),
        P("grp", "row"),
        P("grp", "row"),
        P("grp", "row"),
        P("grp", "row", None),
        P("grp", "row"),
        P("grp", "row"),
    )

    return jax.shard_map(
        local, mesh=mesh, in_specs=placed, out_specs=P("grp", "row", None), check_vma=False
    )
```

profile of v0, /device:TPU:0, one launch (start us, length us, event | category | flops | bytes accessed | tf_op | source)
XLA Modules:
  0.0 26.5 jit_solution(12148902658863560528)
XLA Ops:
  0.0 3.0 %collective-permute-start = (bf16[4,128,256]{2,1,0:T(8,128)(2,1)}, bf16[4,128,256]{2,1,0:T(8,128)(2,1)S(1)}, u32[]{:S(2)}, u32[]{:S(2)}) collective-permute-start(bf16[4,128,256]{2,1,0:T(8,128)(2,1)} %param.9), channel_id=1, source_target_pairs={{0,16},{8,24},{16,0},{24,8},{1,17},{9,25},{17,1},{25,9},{2,18},{10... | collective-permute-start | bytes 786440 | tf_op jit(solution)/shard_map/ppermute | solution.py:200
  3.0 1.5 %shard_map.91 = (bf16[256,256]{1,0:T(8,128)(2,1)S(1)}, bf16[4,256,256]{2,1,0:T(8,128)(2,1)S(1)}, bf16[4,256,256]{2,1,0:T(8,128)(2,1)S(1)}, s32[4,4]{1,0:T(4,128)...) custom-call(bf16[4,256,256]{2,1,0:T(8,128)(2,1)} %amps.3, ...), custom_call_target="tpu_custom_call" | custom-call | flops 67108864 | bytes 16845568 | tf_op jit(solution)/shard_map/pallas_call | solution.py:36
  4.4 0.0 copy-start.1
  4.4 1.6 %collective-permute-start.2 = (bf16[256,256]{1,0:T(8,128)(2,1)S(1)}, bf16[256,256]{1,0:T(8,128)(2,1)S(1)}, u32[]{:S(2)}, u32[]{:S(2)}) collective-permute-start(bf16[256,256]{1,0:T(8,128)(2,1)S(1)} %get-tuple-element.21.refs_0_), channel_id=1, source_target_pairs={{0,1},{1,0},{2,3},{3,2},{4,5},{5,4},{6,7},{7,6},{8,9},{9,8},{10,11... | collective-permute-start | bytes 393224 | tf_op jit(solution)/shard_map/ppermute | solution.py:261
  6.7 0.0 copy-start.5
  6.7 0.5 %shard_map.97 = (bf16[256,256]{1,0:T(8,128)(2,1)S(1)}, bf16[256,256]{1,0:T(8,128)(2,1)S(1)}, bf16[256,256]{1,0:T(8,128)(2,1)S(1)}) custom-call(s32[1,1]{1,0:T(1,128)S(6)} %copy.11.count, bf16[4,256,256]{2,1,0:T(8,128)(2,1)S(1)} %get-tuple-element.22.amps, bf16[4,256,256]{2,1,0:T(8,128)(2,1)S(1)} %get-tuple-element.23.bases), custom_call_target="tpu_custom_call" | custom-call | flops 201326592 | bytes 16777280 | tf_op jit(solution)/shard_map/pallas_call | solution.py:36
  7.2 0.0 copy-done.1
  7.2 0.0 copy-start.2
  7.2 0.0 copy-start.3
  7.2 0.0 copy-start.4
  7.2 0.6 %collective-permute-start.3 = (bf16[256,256]{1,0:T(8,128)(2,1)S(1)}, bf16[256,256]{1,0:T(8,128)(2,1)S(1)}, u32[]{:S(2)}, u32[]{:S(2)}) collective-permute-start(bf16[256,256]{1,0:T(8,128)(2,1)S(1)} %get-tuple-element.24.refs_1_), channel_id=1, source_target_pairs={{0,1},{1,0},{2,3},{3,2},{4,5},{5,4},{6,7},{7,6},{8,9},{9,8},{10,11... | collective-permute-start | bytes 393224 | tf_op jit(solution)/shard_map/ppermute | solution.py:261
  7.8 1.5 %collective-permute-start.4 = (bf16[256,256]{1,0:T(8,128)(2,1)S(1)}, bf16[256,256]{1,0:T(8,128)(2,1)S(1)}, u32[]{:S(2)}, u32[]{:S(2)}) collective-permute-start(bf16[256,256]{1,0:T(8,128)(2,1)S(1)} %get-tuple-element.25.refs_2_), channel_id=1, source_target_pairs={{0,1},{1,0},{2,3},{3,2},{4,5},{5,4},{6,7},{7,6},{8,9},{9,8},{10,11... | collective-permute-start | bytes 393224 | tf_op jit(solution)/shard_map/ppermute | solution.py:261
  9.3 0.5 %collective-permute-start.5 = (bf16[256,256]{1,0:T(8,128)(2,1)S(1)}, bf16[256,256]{1,0:T(8,128)(2,1)S(1)}, u32[]{:S(2)}, u32[]{:S(2)}) collective-permute-start(bf16[256,256]{1,0:T(8,128)(2,1)S(1)} %get-tuple-element.26.refs_3_), channel_id=1, source_target_pairs={{0,1},{1,0},{2,3},{3,2},{4,5},{5,4},{6,7},{7,6},{8,9},{9,8},{10,11... | collective-permute-start | bytes 393224 | tf_op jit(solution)/shard_map/ppermute | solution.py:261
  9.8 0.0 copy-done.5
  9.8 0.0 copy-done.2
  9.9 0.0 copy-done.3
  9.9 0.0 copy-done.4
  9.9 0.0 collective-permute-done
  9.9 0.1 collective-permute-start.1
  10.0 0.0 collective-permute-done.2.refs_4_
  10.0 1.6 %collective-permute-start.6 = (bf16[256,256]{1,0:T(8,128)(2,1)S(1)}, bf16[256,256]{1,0:T(8,128)(2,1)S(1)}, u32[]{:S(2)}, u32[]{:S(2)}) collective-permute-start(bf16[256,256]{1,0:T(8,128)(2,1)S(1)} %collective-permute-done.2.refs_4_), channel_id=1, source_target_pairs={{0,2},{1,7},{2,4},{3,1},{4,6},{5,3},{6,0},{7,5},{8,10},{9,15},{10,... | collective-permute-start | bytes 393224 | tf_op jit(solution)/shard_map/ppermute | solution.py:262
  11.6 2.0 %collective-permute-done.3.refs_5_ = bf16[256,256]{1,0:T(8,128)(2,1)S(1)} collective-permute-done((bf16[256,256]{1,0:T(8,128)(2,1)S(1)}, bf16[256,256]{1,0:T(8,128)(2,1)S(1)}, u32[]{:S(2)}, u32[]{:S(2)}) %collective-permute-start.3) | collective-permute-done | bytes 131104 | tf_op jit(solution)/shard_map/ppermute | solution.py:261
  13.6 1.6 %collective-permute-start.7 = (bf16[256,256]{1,0:T(8,128)(2,1)S(1)}, bf16[256,256]{1,0:T(8,128)(2,1)S(1)}, u32[]{:S(2)}, u32[]{:S(2)}) collective-permute-start(bf16[256,256]{1,0:T(8,128)(2,1)S(1)} %collective-permute-done.3.refs_5_), channel_id=1, source_target_pairs={{0,2},{2,4},{4,6},{6,7},{7,5},{5,3},{3,1},{1,0},{8,10},{10,12},{12... | collective-permute-start | bytes 393224 | tf_op jit(solution)/shard_map/ppermute | solution.py:262
  15.2 1.2 %collective-permute-done.4.refs_6_ = bf16[256,256]{1,0:T(8,128)(2,1)S(1)} collective-permute-done((bf16[256,256]{1,0:T(8,128)(2,1)S(1)}, bf16[256,256]{1,0:T(8,128)(2,1)S(1)}, u32[]{:S(2)}, u32[]{:S(2)}) %collective-permute-start.4) | collective-permute-done | bytes 131104 | tf_op jit(solution)/shard_map/ppermute | solution.py:261
  16.5 1.6 %collective-permute-start.8 = (bf16[256,256]{1,0:T(8,128)(2,1)S(1)}, bf16[256,256]{1,0:T(8,128)(2,1)S(1)}, u32[]{:S(2)}, u32[]{:S(2)}) collective-permute-start(bf16[256,256]{1,0:T(8,128)(2,1)S(1)} %collective-permute-done.4.refs_6_), channel_id=1, source_target_pairs={{0,2},{1,7},{2,4},{3,1},{4,6},{5,3},{6,0},{7,5},{8,10},{9,15},{10,... | collective-permute-start | bytes 393224 | tf_op jit(solution)/shard_map/ppermute | solution.py:262
  18.0 1.2 %collective-permute-done.5.refs_7_ = bf16[256,256]{1,0:T(8,128)(2,1)S(1)} collective-permute-done((bf16[256,256]{1,0:T(8,128)(2,1)S(1)}, bf16[256,256]{1,0:T(8,128)(2,1)S(1)}, u32[]{:S(2)}, u32[]{:S(2)}) %collective-permute-start.5) | collective-permute-done | bytes 131104 | tf_op jit(solution)/shard_map/ppermute | solution.py:261
  19.3 0.3 %collective-permute-start.9 = (bf16[256,256]{1,0:T(8,128)(2,1)S(1)}, bf16[256,256]{1,0:T(8,128)(2,1)S(1)}, u32[]{:S(2)}, u32[]{:S(2)}) collective-permute-start(bf16[256,256]{1,0:T(8,128)(2,1)S(1)} %collective-permute-done.5.refs_7_), channel_id=1, source_target_pairs={{0,2},{2,4},{4,6},{6,7},{7,5},{5,3},{3,1},{1,0},{8,10},{10,12},{12... | collective-permute-start | bytes 393224 | tf_op jit(solution)/shard_map/ppermute | solution.py:262
  19.6 0.1 select_reduce_fusion
  19.8 0.0 collective-permute-done.6.refs_8_
  19.8 2.1 %collective-permute-done.7.refs_9_ = bf16[256,256]{1,0:T(8,128)(2,1)S(1)} collective-permute-done((bf16[256,256]{1,0:T(8,128)(2,1)S(1)}, bf16[256,256]{1,0:T(8,128)(2,1)S(1)}, u32[]{:S(2)}, u32[]{:S(2)}) %collective-permute-start.7) | collective-permute-done | bytes 131104 | tf_op jit(solution)/shard_map/ppermute | solution.py:262
  21.9 1.4 %shard_map.98.sums = f32[4,256,256]{2,1,0:T(8,128)S(1)} custom-call(s32[1,1]{1,0:T(1,128)S(6)} %copy.11.count, f32[48,256]{1,0:T(8,128)S(1)} %reshape.5.weights, bf16[256,256]{1,0:T(8,128)(2,1)} %copy-done.1, bf16[256,256]{1,0:T(8,128)(2,1)} %copy-done.2, bf16[256,256]{1,0:T(8,128)(2,1)} %copy-done.3, bf16[256,256]{1,0:T(8,128)(2,1)} %copy-done.4, ...), custom_call_target="tpu_custom_call" | custom-call | flops 2097152 | bytes 21758016 | tf_op jit(solution)/shard_map/pallas_call | solution.py:36
  23.3 0.0 collective-permute-done.1.refs_1_
  23.3 0.0 copy-start
  23.3 1.9 %shard_map.96.base = f32[4,256,256]{2,1,0:T(8,128)S(1)} custom-call(s32[2,4]{1,0:T(2,128)S(1)} %get-tuple-element.18.orbs, f32[1,4]{1,0:T(1,128)S(1)} %get-tuple-element.19.occ, s32[1,1]{1,0:T(1,128)S(6)} %copy.11.count, f32[4,256]{1,0:T(4,128)S(1)} %get-tuple-element.20.energy, bf16[4,256,256]{2,1,0:T(8,128)(2,1)} %amps.3, ...), custom_call_target="tpu_custom_call" | custom-call | flops 268435456 | bytes 25232192 | tf_op jit(solution)/shard_map/pallas_call | solution.py:36
  25.2 0.0 collective-permute-done.8.refs_0_
  25.2 0.0 collective-permute-done.9.refs_1_
  25.2 0.0 copy-done
  25.2 1.3 %shard_map.99 = f32[4,256,256]{2,1,0:T(8,128)} custom-call(s32[1,1]{1,0:T(1,128)S(6)} %copy.11.count, s32[4,4]{1,0:T(4,128)S(1)} %shard_map.95.token, f32[48,256]{1,0:T(8,128)S(1)} %reshape.5.weights, f32[4,256,256]{2,1,0:T(8,128)S(1)} %shard_map.96.base, bf16[4,256,256]{2,1,0:T(8,128)(2,1)S(1)} %copy-done, f32[4,256,256]{2,1,0:T(8,128)S(1)} %shard_map.98.sums, ...), custom_call_target="tpu_custom_call" | custom-call | flops 268435456 | bytes 46924864 | tf_op jit(solution)/shard_map/pallas_call | solution.py:36
  (9 shorter events, 0.1 us)
Async XLA Ops:
  0.0 9.9 %collective-permute-start = (bf16[4,128,256]{2,1,0:T(8,128)(2,1)}, bf16[4,128,256]{2,1,0:T(8,128)(2,1)S(1)}, u32[]{:S(2)}, u32[]{:S(2)}) collective-permute-start(bf16[4,128,256]{2,1,0:T(8,128)(2,1)} %param.9), channel_id=1, source_target_pairs={{0,16},{8,24},{16,0},{24,8},{1,17},{9,25},{17,1},{25,9},{2,18},{10... | collective-permute-start | bytes 786440 | tf_op jit(solution)/shard_map/ppermute | solution.py:200
  4.4 2.7 %copy-start.1 = (bf16[256,256]{1,0:T(8,128)(2,1)}, bf16[256,256]{1,0:T(8,128)(2,1)S(1)}, u32[]{:S(2)}) copy-start(bf16[256,256]{1,0:T(8,128)(2,1)S(1)} %get-tuple-element.21.refs_0_) | copy-start | bytes 393220
  4.4 5.6 %collective-permute-start.2 = (bf16[256,256]{1,0:T(8,128)(2,1)S(1)}, bf16[256,256]{1,0:T(8,128)(2,1)S(1)}, u32[]{:S(2)}, u32[]{:S(2)}) collective-permute-start(bf16[256,256]{1,0:T(8,128)(2,1)S(1)} %get-tuple-element.21.refs_0_), channel_id=1, source_target_pairs={{0,1},{1,0},{2,3},{3,2},{4,5},{5,4},{6,7},{7,6},{8,9},{9,8},{10,11... | collective-permute-start | bytes 393224 | tf_op jit(solution)/shard_map/ppermute | solution.py:261
  6.7 3.1 %copy-start.5 = (bf16[4,128,256]{2,1,0:T(8,128)(2,1)S(1)}, bf16[4,128,256]{2,1,0:T(8,128)(2,1)}, u32[]{:S(2)}) copy-start(bf16[4,128,256]{2,1,0:T(8,128)(2,1)} %param.9) | copy-start | bytes 786436
  7.2 2.7 %copy-start.2 = (bf16[256,256]{1,0:T(8,128)(2,1)}, bf16[256,256]{1,0:T(8,128)(2,1)S(1)}, u32[]{:S(2)}) copy-start(bf16[256,256]{1,0:T(8,128)(2,1)S(1)} %get-tuple-element.24.refs_1_) | copy-start | bytes 393220
  7.2 2.7 %copy-start.3 = (bf16[256,256]{1,0:T(8,128)(2,1)}, bf16[256,256]{1,0:T(8,128)(2,1)S(1)}, u32[]{:S(2)}) copy-start(bf16[256,256]{1,0:T(8,128)(2,1)S(1)} %get-tuple-element.25.refs_2_) | copy-start | bytes 393220
  7.2 2.7 %copy-start.4 = (bf16[256,256]{1,0:T(8,128)(2,1)}, bf16[256,256]{1,0:T(8,128)(2,1)S(1)}, u32[]{:S(2)}) copy-start(bf16[256,256]{1,0:T(8,128)(2,1)S(1)} %get-tuple-element.26.refs_3_) | copy-start | bytes 393220
  7.2 6.4 %collective-permute-start.3 = (bf16[256,256]{1,0:T(8,128)(2,1)S(1)}, bf16[256,256]{1,0:T(8,128)(2,1)S(1)}, u32[]{:S(2)}, u32[]{:S(2)}) collective-permute-start(bf16[256,256]{1,0:T(8,128)(2,1)S(1)} %get-tuple-element.24.refs_1_), channel_id=1, source_target_pairs={{0,1},{1,0},{2,3},{3,2},{4,5},{5,4},{6,7},{7,6},{8,9},{9,8},{10,11... | collective-permute-start | bytes 393224 | tf_op jit(solution)/shard_map/ppermute | solution.py:261
  7.8 8.7 %collective-permute-start.4 = (bf16[256,256]{1,0:T(8,128)(2,1)S(1)}, bf16[256,256]{1,0:T(8,128)(2,1)S(1)}, u32[]{:S(2)}, u32[]{:S(2)}) collective-permute-start(bf16[256,256]{1,0:T(8,128)(2,1)S(1)} %get-tuple-element.25.refs_2_), channel_id=1, source_target_pairs={{0,1},{1,0},{2,3},{3,2},{4,5},{5,4},{6,7},{7,6},{8,9},{9,8},{10,11... | collective-permute-start | bytes 393224 | tf_op jit(solution)/shard_map/ppermute | solution.py:261
  9.3 10.0 %collective-permute-start.5 = (bf16[256,256]{1,0:T(8,128)(2,1)S(1)}, bf16[256,256]{1,0:T(8,128)(2,1)S(1)}, u32[]{:S(2)}, u32[]{:S(2)}) collective-permute-start(bf16[256,256]{1,0:T(8,128)(2,1)S(1)} %get-tuple-element.26.refs_3_), channel_id=1, source_target_pairs={{0,1},{1,0},{2,3},{3,2},{4,5},{5,4},{6,7},{7,6},{8,9},{9,8},{10,11... | collective-permute-start | bytes 393224 | tf_op jit(solution)/shard_map/ppermute | solution.py:261
  9.9 13.4 %collective-permute-start.1 = (bf16[4,256,256]{2,1,0:T(8,128)(2,1)S(1)}, bf16[4,256,256]{2,1,0:T(8,128)(2,1)S(1)}, u32[]{:S(2)}, u32[]{:S(2)}) collective-permute-start(bf16[4,256,256]{2,1,0:T(8,128)(2,1)S(1)} %constant_dynamic-update-slice_fusion.refs_0_), channel_id=1, source_target_pairs={{0,8},{8,0},{16,24},{24,16},{1,9},{9,1},{17,25},{25,17},{2,10},{10... | collective-permute-start | bytes 1572872 | tf_op jit(solution)/shard_map/ppermute | solution.py:200
  10.0 9.8 %collective-permute-start.6 = (bf16[256,256]{1,0:T(8,128)(2,1)S(1)}, bf16[256,256]{1,0:T(8,128)(2,1)S(1)}, u32[]{:S(2)}, u32[]{:S(2)}) collective-permute-start(bf16[256,256]{1,0:T(8,128)(2,1)S(1)} %collective-permute-done.2.refs_4_), channel_id=1, source_target_pairs={{0,2},{1,7},{2,4},{3,1},{4,6},{5,3},{6,0},{7,5},{8,10},{9,15},{10,... | collective-permute-start | bytes 393224 | tf_op jit(solution)/shard_map/ppermute | solution.py:262
  13.6 8.2 %collective-permute-start.7 = (bf16[256,256]{1,0:T(8,128)(2,1)S(1)}, bf16[256,256]{1,0:T(8,128)(2,1)S(1)}, u32[]{:S(2)}, u32[]{:S(2)}) collective-permute-start(bf16[256,256]{1,0:T(8,128)(2,1)S(1)} %collective-permute-done.3.refs_5_), channel_id=1, source_target_pairs={{0,2},{2,4},{4,6},{6,7},{7,5},{5,3},{3,1},{1,0},{8,10},{10,12},{12... | collective-permute-start | bytes 393224 | tf_op jit(solution)/shard_map/ppermute | solution.py:262
  16.5 8.7 %collective-permute-start.8 = (bf16[256,256]{1,0:T(8,128)(2,1)S(1)}, bf16[256,256]{1,0:T(8,128)(2,1)S(1)}, u32[]{:S(2)}, u32[]{:S(2)}) collective-permute-start(bf16[256,256]{1,0:T(8,128)(2,1)S(1)} %collective-permute-done.4.refs_6_), channel_id=1, source_target_pairs={{0,2},{1,7},{2,4},{3,1},{4,6},{5,3},{6,0},{7,5},{8,10},{9,15},{10,... | collective-permute-start | bytes 393224 | tf_op jit(solution)/shard_map/ppermute | solution.py:262
  19.3 5.9 %collective-permute-start.9 = (bf16[256,256]{1,0:T(8,128)(2,1)S(1)}, bf16[256,256]{1,0:T(8,128)(2,1)S(1)}, u32[]{:S(2)}, u32[]{:S(2)}) collective-permute-start(bf16[256,256]{1,0:T(8,128)(2,1)S(1)} %collective-permute-done.5.refs_7_), channel_id=1, source_target_pairs={{0,2},{2,4},{4,6},{6,7},{7,5},{5,3},{3,1},{1,0},{8,10},{10,12},{12... | collective-permute-start | bytes 393224 | tf_op jit(solution)/shard_map/ppermute | solution.py:262
  23.3 1.9 %copy-start = (bf16[4,256,256]{2,1,0:T(8,128)(2,1)S(1)}, bf16[4,256,256]{2,1,0:T(8,128)(2,1)}, u32[]{:S(2)}) copy-start(bf16[4,256,256]{2,1,0:T(8,128)(2,1)} %bases.3) | copy-start | bytes 1572868
where the time goes:
time: 26.7 us; the launch traced here: 26.5 us
  starting transfers between devices  12.4 us (46%)
  waiting for transfers between devices  6.53 us (24%)
  Pallas kernels  6.52 us (24%)
  between operations  0.86 us (3%)
    pallas_call x9, Pallas kernels, call(): pl.pallas_call(kernel, out_shape=shapes, in_specs=specs, out_specs=out_sp...  6.52 us
    ppermute x4, starting transfers between devices, local(): lax.ppermute(t, 'grp', ring if n in (0, 2) else cycle)  5.13 us
    ppermute x4, waiting for transfers between devices, local(): near = [lax.ppermute(t, 'grp', swap) for t in own]  4.45 us
    ppermute x4, starting transfers between devices, local(): near = [lax.ppermute(t, 'grp', swap) for t in own]  4.18 us
    ppermute x2, starting transfers between devices, row_pieces(): pieces = [piece, lax.ppermute(piece, 'row', pairs)]  3.04 us
    ppermute x4, waiting for transfers between devices, local(): lax.ppermute(t, 'grp', ring if n in (0, 2) else cycle)  2.07 us
  transfers between devices with their start and end apart: 10, of which 4 were waited for; matrix products, arithmetic and copies ran while one was open for 1% of the time, Pallas kernels for 20%

commit v1 on v0

--- a/solution.py
+++ b/solution.py
@@ -202,6 +202,11 @@
     return pieces
 
 
+def whole_pairs(pairs):
+    rows, count = lax.axis_size("row"), lax.axis_size("grp")
+    return [(r * count + i, (r ^ 1 if i == j else r) * count + j) for r in range(rows) for i, j in pairs]
+
+
 def tile_weights(neighbours, coupling, width, virt):
     levels = lax.axis_size("grp") // 2
     group = lax.axis_index("grp")
@@ -257,9 +262,12 @@
     ring = [(i, (i + 2) % count if i % 2 == 0 else (i - 2) % count) for i in range(count)]
     path = list(range(0, count, 2)) + list(range(count - 1, 0, -2))
     cycle = list(zip(path, path[1:] + path[:1]))
+    direct = [(i, i - 1 if i % 2 == 0 else i + 1) for i in range(1, count - 1)]
+    direct = whole_pairs(direct + [(0, 0), (count - 1, count - 1)])
     half = width // 2
     near = [lax.ppermute(t, "grp", swap) for t in own]
-    far = [lax.ppermute(t, "grp", ring if n in (0, 2) else cycle) for n, t in enumerate(near)]
+    far = [lax.ppermute(t, "grp", ring if n < half else cycle) for n, t in enumerate(near[:last])]
+    far.append(lax.ppermute(own[last], ("row", "grp"), direct))
     token = neighbours
     for _ in range(width):
         mark = [(VMEM, token.shape, token.dtype)]

time: 26.7 us -> 26.6 us (level)
  waiting for transfers between devices: 6.53 us -> 5.98 us
  starting transfers between devices: 12.4 us -> 12.8 us
    ppermute x4, waiting for transfers between devices: 2.07 us -> 1.31 us  [the longest x3 1.3 us: local(): lax.ppermute(t, 'grp', ring if n < half else cycle)]
    ppermute x4, starting transfers between devices: 5.13 us -> 5.61 us  [the longest x3 5.61 us: local(): lax.ppermute(t, 'grp', ring if n < half else cycle)]
where the time goes in v1:
time: 26.6 us; the launch traced here: 26.4 us
  starting transfers between devices  12.8 us (48%)
  Pallas kernels  6.52 us (25%)
  waiting for transfers between devices  5.98 us (22%)
  between operations  0.86 us (3%)
    pallas_call x9, Pallas kernels, call(): pl.pallas_call(kernel, out_shape=shapes, in_specs=specs, out_specs=out_sp...  6.52 us
    ppermute x3, starting transfers between devices, local(): lax.ppermute(t, 'grp', ring if n < half else cycle)  5.61 us
    ppermute x4, waiting for transfers between devices, local(): near = [lax.ppermute(t, 'grp', swap) for t in own]  4.67 us
    ppermute x4, starting transfers between devices, local(): near = [lax.ppermute(t, 'grp', swap) for t in own]  4.18 us
    ppermute x2, starting transfers between devices, row_pieces(): pieces = [piece, lax.ppermute(piece, 'row', pairs)]  3.04 us
    ppermute x3, waiting for transfers between devices, local(): lax.ppermute(t, 'grp', ring if n < half else cycle)  1.3 us
  transfers between devices with their start and end apart: 10, of which 4 were waited for; matrix products, arithmetic and copies ran while one was open for 1% of the time, Pallas kernels for 20%

profile of v1, /device:TPU:0, one launch (start us, length us, event | category | flops | bytes accessed | tf_op | source)
XLA Modules:
  0.0 26.4 jit_solution(6717480952994485298)
XLA Ops:
  0.0 3.0 %collective-permute-start = (bf16[4,128,256]{2,1,0:T(8,128)(2,1)}, bf16[4,128,256]{2,1,0:T(8,128)(2,1)S(1)}, u32[]{:S(2)}, u32[]{:S(2)}) collective-permute-start(bf16[4,128,256]{2,1,0:T(8,128)(2,1)} %param.9), channel_id=1, source_target_pairs={{0,16},{8,24},{16,0},{24,8},{1,17},{9,25},{17,1},{25,9},{2,18},{10... | collective-permute-start | bytes 786440 | tf_op jit(solution)/shard_map/ppermute | solution.py:200
  3.0 1.5 %shard_map.91 = (bf16[256,256]{1,0:T(8,128)(2,1)S(1)}, bf16[4,256,256]{2,1,0:T(8,128)(2,1)S(1)}, bf16[4,256,256]{2,1,0:T(8,128)(2,1)S(1)}, s32[4,4]{1,0:T(4,128)...) custom-call(bf16[4,256,256]{2,1,0:T(8,128)(2,1)} %amps.3, ...), custom_call_target="tpu_custom_call" | custom-call | flops 67108864 | bytes 16845568 | tf_op jit(solution)/shard_map/pallas_call | solution.py:36
  4.4 0.0 copy-start.2
  4.4 1.6 %collective-permute-start.2 = (bf16[256,256]{1,0:T(8,128)(2,1)S(1)}, bf16[256,256]{1,0:T(8,128)(2,1)S(1)}, u32[]{:S(2)}, u32[]{:S(2)}) collective-permute-start(bf16[256,256]{1,0:T(8,128)(2,1)S(1)} %get-tuple-element.21.refs_0_), channel_id=1, source_target_pairs={{0,1},{1,0},{2,3},{3,2},{4,5},{5,4},{6,7},{7,6},{8,9},{9,8},{10,11... | collective-permute-start | bytes 393224 | tf_op jit(solution)/shard_map/ppermute | solution.py:268
  6.7 0.0 copy-start.5
  6.7 0.5 %shard_map.97 = (bf16[256,256]{1,0:T(8,128)(2,1)S(1)}, bf16[256,256]{1,0:T(8,128)(2,1)S(1)}, bf16[256,256]{1,0:T(8,128)(2,1)S(1)}) custom-call(s32[1,1]{1,0:T(1,128)S(6)} %copy.11.count, bf16[4,256,256]{2,1,0:T(8,128)(2,1)S(1)} %get-tuple-element.22.amps, bf16[4,256,256]{2,1,0:T(8,128)(2,1)S(1)} %get-tuple-element.23.bases), custom_call_target="tpu_custom_call" | custom-call | flops 201326592 | bytes 16777280 | tf_op jit(solution)/shard_map/pallas_call | solution.py:36
  7.2 0.0 copy-done.2
  7.2 0.0 copy-start.3
  7.2 0.0 copy-start.4
  7.2 0.0 copy-start.1
  7.2 0.6 %collective-permute-start.3 = (bf16[256,256]{1,0:T(8,128)(2,1)S(1)}, bf16[256,256]{1,0:T(8,128)(2,1)S(1)}, u32[]{:S(2)}, u32[]{:S(2)}) collective-permute-start(bf16[256,256]{1,0:T(8,128)(2,1)S(1)} %get-tuple-element.24.refs_1_), channel_id=1, source_target_pairs={{0,1},{1,0},{2,3},{3,2},{4,5},{5,4},{6,7},{7,6},{8,9},{9,8},{10,11... | collective-permute-start | bytes 393224 | tf_op jit(solution)/shard_map/ppermute | solution.py:268
  7.8 1.5 %collective-permute-start.4 = (bf16[256,256]{1,0:T(8,128)(2,1)S(1)}, bf16[256,256]{1,0:T(8,128)(2,1)S(1)}, u32[]{:S(2)}, u32[]{:S(2)}) collective-permute-start(bf16[256,256]{1,0:T(8,128)(2,1)S(1)} %get-tuple-element.25.refs_2_), channel_id=1, source_target_pairs={{0,1},{1,0},{2,3},{3,2},{4,5},{5,4},{6,7},{7,6},{8,9},{9,8},{10,11... | collective-permute-start | bytes 393224 | tf_op jit(solution)/shard_map/ppermute | solution.py:268
  9.3 0.5 %collective-permute-start.5 = (bf16[256,256]{1,0:T(8,128)(2,1)S(1)}, bf16[256,256]{1,0:T(8,128)(2,1)S(1)}, u32[]{:S(2)}, u32[]{:S(2)}) collective-permute-start(bf16[256,256]{1,0:T(8,128)(2,1)S(1)} %get-tuple-element.26.refs_3_), channel_id=1, source_target_pairs={{0,1},{1,0},{2,3},{3,2},{4,5},{5,4},{6,7},{7,6},{8,9},{9,8},{10,11... | collective-permute-start | bytes 393224 | tf_op jit(solution)/shard_map/ppermute | solution.py:268
  9.8 0.0 copy-done.5
  9.8 0.0 copy-done.3
  9.9 0.0 copy-done.4
  9.9 0.0 collective-permute-done
  9.9 0.1 collective-permute-start.1
  10.0 0.0 collective-permute-done.2.refs_4_
  10.0 1.6 %collective-permute-start.6 = (bf16[256,256]{1,0:T(8,128)(2,1)S(1)}, bf16[256,256]{1,0:T(8,128)(2,1)S(1)}, u32[]{:S(2)}, u32[]{:S(2)}) collective-permute-start(bf16[256,256]{1,0:T(8,128)(2,1)S(1)} %collective-permute-done.2.refs_4_), channel_id=1, source_target_pairs={{0,2},{1,7},{2,4},{3,1},{4,6},{5,3},{6,0},{7,5},{8,10},{9,15},{10,... | collective-permute-start | bytes 393224 | tf_op jit(solution)/shard_map/ppermute | solution.py:269
  11.6 2.0 %collective-permute-done.3.refs_5_ = bf16[256,256]{1,0:T(8,128)(2,1)S(1)} collective-permute-done((bf16[256,256]{1,0:T(8,128)(2,1)S(1)}, bf16[256,256]{1,0:T(8,128)(2,1)S(1)}, u32[]{:S(2)}, u32[]{:S(2)}) %collective-permute-start.3) | collective-permute-done | bytes 131104 | tf_op jit(solution)/shard_map/ppermute | solution.py:268
  13.6 1.6 %collective-permute-start.7 = (bf16[256,256]{1,0:T(8,128)(2,1)S(1)}, bf16[256,256]{1,0:T(8,128)(2,1)S(1)}, u32[]{:S(2)}, u32[]{:S(2)}) collective-permute-start(bf16[256,256]{1,0:T(8,128)(2,1)S(1)} %collective-permute-done.3.refs_5_), channel_id=1, source_target_pairs={{0,2},{1,7},{2,4},{3,1},{4,6},{5,3},{6,0},{7,5},{8,10},{9,15},{10,... | collective-permute-start | bytes 393224 | tf_op jit(solution)/shard_map/ppermute | solution.py:269
  15.2 1.2 %collective-permute-done.4.refs_6_ = bf16[256,256]{1,0:T(8,128)(2,1)S(1)} collective-permute-done((bf16[256,256]{1,0:T(8,128)(2,1)S(1)}, bf16[256,256]{1,0:T(8,128)(2,1)S(1)}, u32[]{:S(2)}, u32[]{:S(2)}) %collective-permute-start.4) | collective-permute-done | bytes 131104 | tf_op jit(solution)/shard_map/ppermute | solution.py:268
  16.5 0.0 copy-done.1
  16.5 0.0 collective-permute-start.9
  16.5 1.4 %collective-permute-done.5.refs_7_ = bf16[256,256]{1,0:T(8,128)(2,1)S(1)} collective-permute-done((bf16[256,256]{1,0:T(8,128)(2,1)S(1)}, bf16[256,256]{1,0:T(8,128)(2,1)S(1)}, u32[]{:S(2)}, u32[]{:S(2)}) %collective-permute-start.5) | collective-permute-done | bytes 131104 | tf_op jit(solution)/shard_map/ppermute | solution.py:268
  17.9 2.4 %collective-permute-start.8 = (bf16[256,256]{1,0:T(8,128)(2,1)S(1)}, bf16[256,256]{1,0:T(8,128)(2,1)S(1)}, u32[]{:S(2)}, u32[]{:S(2)}) collective-permute-start(bf16[256,256]{1,0:T(8,128)(2,1)S(1)} %collective-permute-done.4.refs_6_), channel_id=1, source_target_pairs={{0,2},{2,4},{4,6},{6,7},{7,5},{5,3},{3,1},{1,0},{8,10},{10,12},{12... | collective-permute-start | bytes 393224 | tf_op jit(solution)/shard_map/ppermute | solution.py:269
  20.3 0.1 select_reduce_fusion
  20.5 0.0 collective-permute-done.6.refs_8_
  20.5 1.3 %collective-permute-done.7.refs_9_ = bf16[256,256]{1,0:T(8,128)(2,1)S(1)} collective-permute-done((bf16[256,256]{1,0:T(8,128)(2,1)S(1)}, bf16[256,256]{1,0:T(8,128)(2,1)S(1)}, u32[]{:S(2)}, u32[]{:S(2)}) %collective-permute-start.7) | collective-permute-done | bytes 131104 | tf_op jit(solution)/shard_map/ppermute | solution.py:269
  21.8 1.4 %shard_map.98.sums = f32[4,256,256]{2,1,0:T(8,128)S(1)} custom-call(s32[1,1]{1,0:T(1,128)S(6)} %copy.11.count, f32[48,256]{1,0:T(8,128)S(1)} %reshape.5.weights, bf16[256,256]{1,0:T(8,128)(2,1)} %copy-done.2, bf16[256,256]{1,0:T(8,128)(2,1)} %copy-done.3, bf16[256,256]{1,0:T(8,128)(2,1)} %copy-done.4, bf16[256,256]{1,0:T(8,128)(2,1)} %copy-done.1, ...), custom_call_target="tpu_custom_call" | custom-call | flops 2097152 | bytes 21758016 | tf_op jit(solution)/shard_map/pallas_call | solution.py:36
  23.2 0.0 collective-permute-done.1.refs_1_
  23.2 0.0 copy-start
  23.2 1.9 %shard_map.96.base = f32[4,256,256]{2,1,0:T(8,128)S(1)} custom-call(s32[2,4]{1,0:T(2,128)S(1)} %get-tuple-element.18.orbs, f32[1,4]{1,0:T(1,128)S(1)} %get-tuple-element.19.occ, s32[1,1]{1,0:T(1,128)S(6)} %copy.11.count, f32[4,256]{1,0:T(4,128)S(1)} %get-tuple-element.20.energy, bf16[4,256,256]{2,1,0:T(8,128)(2,1)} %amps.3, ...), custom_call_target="tpu_custom_call" | custom-call | flops 268435456 | bytes 25232192 | tf_op jit(solution)/shard_map/pallas_call | solution.py:36
  25.1 0.0 collective-permute-done.9.refs_1_
  25.1 0.0 collective-permute-done.8.refs_0_
  25.1 0.0 copy-done
  25.1 1.3 %shard_map.99 = f32[4,256,256]{2,1,0:T(8,128)} custom-call(s32[1,1]{1,0:T(1,128)S(6)} %copy.11.count, s32[4,4]{1,0:T(4,128)S(1)} %shard_map.95.token, f32[48,256]{1,0:T(8,128)S(1)} %reshape.5.weights, f32[4,256,256]{2,1,0:T(8,128)S(1)} %shard_map.96.base, bf16[4,256,256]{2,1,0:T(8,128)(2,1)S(1)} %copy-done, f32[4,256,256]{2,1,0:T(8,128)S(1)} %shard_map.98.sums, ...), custom_call_target="tpu_custom_call" | custom-call | flops 268435456 | bytes 46924864 | tf_op jit(solution)/shard_map/pallas_call | solution.py:36
  (9 shorter events, 0.1 us)
Async XLA Ops:
  0.0 9.9 %collective-permute-start = (bf16[4,128,256]{2,1,0:T(8,128)(2,1)}, bf16[4,128,256]{2,1,0:T(8,128)(2,1)S(1)}, u32[]{:S(2)}, u32[]{:S(2)}) collective-permute-start(bf16[4,128,256]{2,1,0:T(8,128)(2,1)} %param.9), channel_id=1, source_target_pairs={{0,16},{8,24},{16,0},{24,8},{1,17},{9,25},{17,1},{25,9},{2,18},{10... | collective-permute-start | bytes 786440 | tf_op jit(solution)/shard_map/ppermute | solution.py:200
  4.4 2.7 %copy-start.2 = (bf16[256,256]{1,0:T(8,128)(2,1)}, bf16[256,256]{1,0:T(8,128)(2,1)S(1)}, u32[]{:S(2)}) copy-start(bf16[256,256]{1,0:T(8,128)(2,1)S(1)} %get-tuple-element.21.refs_0_) | copy-start | bytes 393220
  4.4 5.6 %collective-permute-start.2 = (bf16[256,256]{1,0:T(8,128)(2,1)S(1)}, bf16[256,256]{1,0:T(8,128)(2,1)S(1)}, u32[]{:S(2)}, u32[]{:S(2)}) collective-permute-start(bf16[256,256]{1,0:T(8,128)(2,1)S(1)} %get-tuple-element.21.refs_0_), channel_id=1, source_target_pairs={{0,1},{1,0},{2,3},{3,2},{4,5},{5,4},{6,7},{7,6},{8,9},{9,8},{10,11... | collective-permute-start | bytes 393224 | tf_op jit(solution)/shard_map/ppermute | solution.py:268
  6.7 3.1 %copy-start.5 = (bf16[4,128,256]{2,1,0:T(8,128)(2,1)S(1)}, bf16[4,128,256]{2,1,0:T(8,128)(2,1)}, u32[]{:S(2)}) copy-start(bf16[4,128,256]{2,1,0:T(8,128)(2,1)} %param.9) | copy-start | bytes 786436
  7.2 2.7 %copy-start.3 = (bf16[256,256]{1,0:T(8,128)(2,1)}, bf16[256,256]{1,0:T(8,128)(2,1)S(1)}, u32[]{:S(2)}) copy-start(bf16[256,256]{1,0:T(8,128)(2,1)S(1)} %get-tuple-element.24.refs_1_) | copy-start | bytes 393220
  7.2 2.7 %copy-start.4 = (bf16[256,256]{1,0:T(8,128)(2,1)}, bf16[256,256]{1,0:T(8,128)(2,1)S(1)}, u32[]{:S(2)}) copy-start(bf16[256,256]{1,0:T(8,128)(2,1)S(1)} %get-tuple-element.25.refs_2_) | copy-start | bytes 393220
  7.2 9.3 %copy-start.1 = (bf16[256,256]{1,0:T(8,128)(2,1)}, bf16[256,256]{1,0:T(8,128)(2,1)S(1)}, u32[]{:S(2)}) copy-start(bf16[256,256]{1,0:T(8,128)(2,1)S(1)} %get-tuple-element.26.refs_3_) | copy-start | bytes 393220
  7.2 6.4 %collective-permute-start.3 = (bf16[256,256]{1,0:T(8,128)(2,1)S(1)}, bf16[256,256]{1,0:T(8,128)(2,1)S(1)}, u32[]{:S(2)}, u32[]{:S(2)}) collective-permute-start(bf16[256,256]{1,0:T(8,128)(2,1)S(1)} %get-tuple-element.24.refs_1_), channel_id=1, source_target_pairs={{0,1},{1,0},{2,3},{3,2},{4,5},{5,4},{6,7},{7,6},{8,9},{9,8},{10,11... | collective-permute-start | bytes 393224 | tf_op jit(solution)/shard_map/ppermute | solution.py:268
  7.8 8.7 %collective-permute-start.4 = (bf16[256,256]{1,0:T(8,128)(2,1)S(1)}, bf16[256,256]{1,0:T(8,128)(2,1)S(1)}, u32[]{:S(2)}, u32[]{:S(2)}) collective-permute-start(bf16[256,256]{1,0:T(8,128)(2,1)S(1)} %get-tuple-element.25.refs_2_), channel_id=1, source_target_pairs={{0,1},{1,0},{2,3},{3,2},{4,5},{5,4},{6,7},{7,6},{8,9},{9,8},{10,11... | collective-permute-start | bytes 393224 | tf_op jit(solution)/shard_map/ppermute | solution.py:268
  9.3 8.6 %collective-permute-start.5 = (bf16[256,256]{1,0:T(8,128)(2,1)S(1)}, bf16[256,256]{1,0:T(8,128)(2,1)S(1)}, u32[]{:S(2)}, u32[]{:S(2)}) collective-permute-start(bf16[256,256]{1,0:T(8,128)(2,1)S(1)} %get-tuple-element.26.refs_3_), channel_id=1, source_target_pairs={{0,1},{1,0},{2,3},{3,2},{4,5},{5,4},{6,7},{7,6},{8,9},{9,8},{10,11... | collective-permute-start | bytes 393224 | tf_op jit(solution)/shard_map/ppermute | solution.py:268
  9.9 13.3 %collective-permute-start.1 = (bf16[4,256,256]{2,1,0:T(8,128)(2,1)S(1)}, bf16[4,256,256]{2,1,0:T(8,128)(2,1)S(1)}, u32[]{:S(2)}, u32[]{:S(2)}) collective-permute-start(bf16[4,256,256]{2,1,0:T(8,128)(2,1)S(1)} %constant_dynamic-update-slice_fusion.refs_0_), channel_id=1, source_target_pairs={{0,8},{8,0},{16,24},{24,16},{1,9},{9,1},{17,25},{25,17},{2,10},{10... | collective-permute-start | bytes 1572872 | tf_op jit(solution)/shard_map/ppermute | solution.py:200
  10.0 10.5 %collective-permute-start.6 = (bf16[256,256]{1,0:T(8,128)(2,1)S(1)}, bf16[256,256]{1,0:T(8,128)(2,1)S(1)}, u32[]{:S(2)}, u32[]{:S(2)}) collective-permute-start(bf16[256,256]{1,0:T(8,128)(2,1)S(1)} %collective-permute-done.2.refs_4_), channel_id=1, source_target_pairs={{0,2},{1,7},{2,4},{3,1},{4,6},{5,3},{6,0},{7,5},{8,10},{9,15},{10,... | collective-permute-start | bytes 393224 | tf_op jit(solution)/shard_map/ppermute | solution.py:269
  13.6 8.1 %collective-permute-start.7 = (bf16[256,256]{1,0:T(8,128)(2,1)S(1)}, bf16[256,256]{1,0:T(8,128)(2,1)S(1)}, u32[]{:S(2)}, u32[]{:S(2)}) collective-permute-start(bf16[256,256]{1,0:T(8,128)(2,1)S(1)} %collective-permute-done.3.refs_5_), channel_id=1, source_target_pairs={{0,2},{1,7},{2,4},{3,1},{4,6},{5,3},{6,0},{7,5},{8,10},{9,15},{10,... | collective-permute-start | bytes 393224 | tf_op jit(solution)/shard_map/ppermute | solution.py:269
  16.5 8.7 %collective-permute-start.9 = (bf16[256,256]{1,0:T(8,128)(2,1)S(1)}, bf16[256,256]{1,0:T(8,128)(2,1)S(1)}, u32[]{:S(2)}, u32[]{:S(2)}) collective-permute-start(bf16[256,256]{1,0:T(8,128)(2,1)S(1)} %get-tuple-element.26.refs_3_), channel_id=1, source_target_pairs={{1,2},{2,1},{3,4},{4,3},{5,6},{6,5},{0,8},{7,15},{9,10},{10,9},{11... | collective-permute-start | bytes 393224 | tf_op jit(solution)/shard_map/ppermute | solution.py:270
  17.9 7.2 %collective-permute-start.8 = (bf16[256,256]{1,0:T(8,128)(2,1)S(1)}, bf16[256,256]{1,0:T(8,128)(2,1)S(1)}, u32[]{:S(2)}, u32[]{:S(2)}) collective-permute-start(bf16[256,256]{1,0:T(8,128)(2,1)S(1)} %collective-permute-done.4.refs_6_), channel_id=1, source_target_pairs={{0,2},{2,4},{4,6},{6,7},{7,5},{5,3},{3,1},{1,0},{8,10},{10,12},{12... | collective-permute-start | bytes 393224 | tf_op jit(solution)/shard_map/ppermute | solution.py:269
  23.2 1.9 %copy-start = (bf16[4,256,256]{2,1,0:T(8,128)(2,1)S(1)}, bf16[4,256,256]{2,1,0:T(8,128)(2,1)}, u32[]{:S(2)}) copy-start(bf16[4,256,256]{2,1,0:T(8,128)(2,1)} %bases.3) | copy-start | bytes 1572868

commit v2 on v1

--- a/solution.py
+++ b/solution.py
@@ -157,13 +157,22 @@
     width = base.shape[0]
     half = width // 2
     total = weights.shape[0] // width
-    stores = [pltpu.make_async_copy(held.at[s], out.at[s], sems.at[s]) for s in range(width)]
+    parts = sems.shape[1]
+    height = base.shape[1] // parts
+    stores = []
+    for slot in range(width):
+        cuts = [(slot, pl.ds(part * height, height)) for part in range(parts)]
+        stores.append([
+            pltpu.make_async_copy(held.at[cut], out.at[cut], sems.at[slot, part])
+            for part, cut in enumerate(cuts)
+        ])
 
     @pl.when(count[0, 0] <= half)
     def _():
         for slot in range(half, width):
             held[slot] = jnp.zeros(held.shape[1:], F32)
-            stores[slot].start()
+            for store in stores[slot]:
+                store.start()
 
     def some(slots):
         combined = []
@@ -175,13 +184,15 @@
             combined.append(acc.astype(BF16))
         firsts = [dot(bases[s], c, ((0,), (0,))).astype(BF16) for s, c in zip(slots, combined)]
         for slot, first in zip(slots, firsts):
-            back = dot(first, bases[slot], ((1,), (0,)))
-            value = base[slot] - back
-            held[slot] = jnp.where(slot < count[0, 0], value, jnp.float32(0))
-            stores[slot].start()
+            for part in range(parts):
+                rows = pl.ds(part * height, height)
+                piece = first[part * height : (part + 1) * height]
+                value = base[slot, rows] - dot(piece, bases[slot], ((1,), (0,)))
+                held[slot, rows] = jnp.where(slot < count[0, 0], value, jnp.float32(0))
+                stores[slot][part].start()
 
     in_halves(count, width, some)
-    for store in stores:
+    for store in sum(stores, []):
         store.wait()
 
 
@@ -293,7 +304,7 @@
         [(pl.ANY, (width, virt, virt), F32)],
         [(SMEM, pair_count), (VMEM, token), (VMEM, weights), (VMEM, base), (VMEM, bases), (VMEM, sums)]
         + [(VMEM, t) for t in far[half:]],
-        2 * width * cube, [VMEM((width, virt, virt), F32), dma((width,))],
+        2 * width * cube, [VMEM((width, virt, virt), F32), dma((width, 2))],
     )[0]
 
 

time: 26.6 us -> 26.6 us (level)
  no operation moved by 1% of the time
where the time goes in v2:
time: 26.6 us; the launch traced here: 26.4 us
  starting transfers between devices  12.8 us (48%)
  Pallas kernels  6.48 us (24%)
  waiting for transfers between devices  5.98 us (22%)
  between operations  0.86 us (3%)
    pallas_call x9, Pallas kernels, call(): pl.pallas_call(kernel, out_shape=shapes, in_specs=specs, out_specs=out_sp...  6.48 us
    ppermute x3, starting transfers between devices, local(): lax.ppermute(t, 'grp', ring if n < half else cycle)  5.61 us
    ppermute x4, waiting for transfers between devices, local(): near = [lax.ppermute(t, 'grp', swap) for t in own]  4.67 us
    ppermute x4, starting transfers between devices, local(): near = [lax.ppermute(t, 'grp', swap) for t in own]  4.18 us
    ppermute x2, starting transfers between devices, row_pieces(): pieces = [piece, lax.ppermute(piece, 'row', pairs)]  3.04 us
    ppermute x3, waiting for transfers between devices, local(): lax.ppermute(t, 'grp', ring if n < half else cycle)  1.3 us
  transfers between devices with their start and end apart: 10, of which 4 were waited for; matrix products, arithmetic and copies ran while one was open for 1% of the time, Pallas kernels for 20%

profile of v2, /device:TPU:0, one launch (start us, length us, event | category | flops | bytes accessed | tf_op | source)
XLA Modules:
  0.0 26.4 jit_solution(15195934419686658035)
XLA Ops:
  0.0 3.0 %collective-permute-start = (bf16[4,128,256]{2,1,0:T(8,128)(2,1)}, bf16[4,128,256]{2,1,0:T(8,128)(2,1)S(1)}, u32[]{:S(2)}, u32[]{:S(2)}) collective-permute-start(bf16[4,128,256]{2,1,0:T(8,128)(2,1)} %param.9), channel_id=1, source_target_pairs={{0,16},{8,24},{16,0},{24,8},{1,17},{9,25},{17,1},{25,9},{2,18},{10... | collective-permute-start | bytes 786440 | tf_op jit(solution)/shard_map/ppermute | solution.py:211
  3.0 1.5 %shard_map.91 = (bf16[256,256]{1,0:T(8,128)(2,1)S(1)}, bf16[4,256,256]{2,1,0:T(8,128)(2,1)S(1)}, bf16[4,256,256]{2,1,0:T(8,128)(2,1)S(1)}, s32[4,4]{1,0:T(4,128)...) custom-call(bf16[4,256,256]{2,1,0:T(8,128)(2,1)} %amps.3, ...), custom_call_target="tpu_custom_call" | custom-call | flops 67108864 | bytes 16845568 | tf_op jit(solution)/shard_map/pallas_call | solution.py:36
  4.4 0.0 copy-start.2
  4.4 1.6 %collective-permute-start.2 = (bf16[256,256]{1,0:T(8,128)(2,1)S(1)}, bf16[256,256]{1,0:T(8,128)(2,1)S(1)}, u32[]{:S(2)}, u32[]{:S(2)}) collective-permute-start(bf16[256,256]{1,0:T(8,128)(2,1)S(1)} %get-tuple-element.21.refs_0_), channel_id=1, source_target_pairs={{0,1},{1,0},{2,3},{3,2},{4,5},{5,4},{6,7},{7,6},{8,9},{9,8},{10,11... | collective-permute-start | bytes 393224 | tf_op jit(solution)/shard_map/ppermute | solution.py:279
  6.7 0.0 copy-start.5
  6.7 0.5 %shard_map.97 = (bf16[256,256]{1,0:T(8,128)(2,1)S(1)}, bf16[256,256]{1,0:T(8,128)(2,1)S(1)}, bf16[256,256]{1,0:T(8,128)(2,1)S(1)}) custom-call(s32[1,1]{1,0:T(1,128)S(6)} %copy.11.count, bf16[4,256,256]{2,1,0:T(8,128)(2,1)S(1)} %get-tuple-element.22.amps, bf16[4,256,256]{2,1,0:T(8,128)(2,1)S(1)} %get-tuple-element.23.bases), custom_call_target="tpu_custom_call" | custom-call | flops 201326592 | bytes 16777280 | tf_op jit(solution)/shard_map/pallas_call | solution.py:36
  7.2 0.0 copy-done.2
  7.2 0.0 copy-start.3
  7.2 0.0 copy-start.4
  7.2 0.0 copy-start.1
  7.2 0.6 %collective-permute-start.3 = (bf16[256,256]{1,0:T(8,128)(2,1)S(1)}, bf16[256,256]{1,0:T(8,128)(2,1)S(1)}, u32[]{:S(2)}, u32[]{:S(2)}) collective-permute-start(bf16[256,256]{1,0:T(8,128)(2,1)S(1)} %get-tuple-element.24.refs_1_), channel_id=1, source_target_pairs={{0,1},{1,0},{2,3},{3,2},{4,5},{5,4},{6,7},{7,6},{8,9},{9,8},{10,11... | collective-permute-start | bytes 393224 | tf_op jit(solution)/shard_map/ppermute | solution.py:279
  7.8 1.5 %collective-permute-start.4 = (bf16[256,256]{1,0:T(8,128)(2,1)S(1)}, bf16[256,256]{1,0:T(8,128)(2,1)S(1)}, u32[]{:S(2)}, u32[]{:S(2)}) collective-permute-start(bf16[256,256]{1,0:T(8,128)(2,1)S(1)} %get-tuple-element.25.refs_2_), channel_id=1, source_target_pairs={{0,1},{1,0},{2,3},{3,2},{4,5},{5,4},{6,7},{7,6},{8,9},{9,8},{10,11... | collective-permute-start | bytes 393224 | tf_op jit(solution)/shard_map/ppermute | solution.py:279
  9.3 0.5 %collective-permute-start.5 = (bf16[256,256]{1,0:T(8,128)(2,1)S(1)}, bf16[256,256]{1,0:T(8,128)(2,1)S(1)}, u32[]{:S(2)}, u32[]{:S(2)}) collective-permute-start(bf16[256,256]{1,0:T(8,128)(2,1)S(1)} %get-tuple-element.26.refs_3_), channel_id=1, source_target_pairs={{0,1},{1,0},{2,3},{3,2},{4,5},{5,4},{6,7},{7,6},{8,9},{9,8},{10,11... | collective-permute-start | bytes 393224 | tf_op jit(solution)/shard_map/ppermute | solution.py:279
  9.8 0.0 copy-done.5
  9.8 0.0 copy-done.3
  9.9 0.0 copy-done.4
  9.9 0.0 collective-permute-done
  9.9 0.1 collective-permute-start.1
  10.0 0.0 collective-permute-done.2.refs_4_
  10.0 1.6 %collective-permute-start.6 = (bf16[256,256]{1,0:T(8,128)(2,1)S(1)}, bf16[256,256]{1,0:T(8,128)(2,1)S(1)}, u32[]{:S(2)}, u32[]{:S(2)}) collective-permute-start(bf16[256,256]{1,0:T(8,128)(2,1)S(1)} %collective-permute-done.2.refs_4_), channel_id=1, source_target_pairs={{0,2},{1,7},{2,4},{3,1},{4,6},{5,3},{6,0},{7,5},{8,10},{9,15},{10,... | collective-permute-start | bytes 393224 | tf_op jit(solution)/shard_map/ppermute | solution.py:280
  11.6 2.0 %collective-permute-done.3.refs_5_ = bf16[256,256]{1,0:T(8,128)(2,1)S(1)} collective-permute-done((bf16[256,256]{1,0:T(8,128)(2,1)S(1)}, bf16[256,256]{1,0:T(8,128)(2,1)S(1)}, u32[]{:S(2)}, u32[]{:S(2)}) %collective-permute-start.3) | collective-permute-done | bytes 131104 | tf_op jit(solution)/shard_map/ppermute | solution.py:279
  13.6 1.6 %collective-permute-start.7 = (bf16[256,256]{1,0:T(8,128)(2,1)S(1)}, bf16[256,256]{1,0:T(8,128)(2,1)S(1)}, u32[]{:S(2)}, u32[]{:S(2)}) collective-permute-start(bf16[256,256]{1,0:T(8,128)(2,1)S(1)} %collective-permute-done.3.refs_5_), channel_id=1, source_target_pairs={{0,2},{1,7},{2,4},{3,1},{4,6},{5,3},{6,0},{7,5},{8,10},{9,15},{10,... | collective-permute-start | bytes 393224 | tf_op jit(solution)/shard_map/ppermute | solution.py:280
  15.2 1.2 %collective-permute-done.4.refs_6_ = bf16[256,256]{1,0:T(8,128)(2,1)S(1)} collective-permute-done((bf16[256,256]{1,0:T(8,128)(2,1)S(1)}, bf16[256,256]{1,0:T(8,128)(2,1)S(1)}, u32[]{:S(2)}, u32[]{:S(2)}) %collective-permute-start.4) | collective-permute-done | bytes 131104 | tf_op jit(solution)/shard_map/ppermute | solution.py:279
  16.5 0.0 copy-done.1
  16.5 0.0 collective-permute-start.9
  16.5 1.4 %collective-permute-done.5.refs_7_ = bf16[256,256]{1,0:T(8,128)(2,1)S(1)} collective-permute-done((bf16[256,256]{1,0:T(8,128)(2,1)S(1)}, bf16[256,256]{1,0:T(8,128)(2,1)S(1)}, u32[]{:S(2)}, u32[]{:S(2)}) %collective-permute-start.5) | collective-permute-done | bytes 131104 | tf_op jit(solution)/shard_map/ppermute | solution.py:279
  17.9 2.4 %collective-permute-start.8 = (bf16[256,256]{1,0:T(8,128)(2,1)S(1)}, bf16[256,256]{1,0:T(8,128)(2,1)S(1)}, u32[]{:S(2)}, u32[]{:S(2)}) collective-permute-start(bf16[256,256]{1,0:T(8,128)(2,1)S(1)} %collective-permute-done.4.refs_6_), channel_id=1, source_target_pairs={{0,2},{2,4},{4,6},{6,7},{7,5},{5,3},{3,1},{1,0},{8,10},{10,12},{12... | collective-permute-start | bytes 393224 | tf_op jit(solution)/shard_map/ppermute | solution.py:280
  20.3 0.1 select_reduce_fusion
  20.5 0.0 collective-permute-done.6.refs_8_
  20.5 1.3 %collective-permute-done.7.refs_9_ = bf16[256,256]{1,0:T(8,128)(2,1)S(1)} collective-permute-done((bf16[256,256]{1,0:T(8,128)(2,1)S(1)}, bf16[256,256]{1,0:T(8,128)(2,1)S(1)}, u32[]{:S(2)}, u32[]{:S(2)}) %collective-permute-start.7) | collective-permute-done | bytes 131104 | tf_op jit(solution)/shard_map/ppermute | solution.py:280
  21.8 1.4 %shard_map.98.sums = f32[4,256,256]{2,1,0:T(8,128)S(1)} custom-call(s32[1,1]{1,0:T(1,128)S(6)} %copy.11.count, f32[48,256]{1,0:T(8,128)S(1)} %reshape.5.weights, bf16[256,256]{1,0:T(8,128)(2,1)} %copy-done.2, bf16[256,256]{1,0:T(8,128)(2,1)} %copy-done.3, bf16[256,256]{1,0:T(8,128)(2,1)} %copy-done.4, bf16[256,256]{1,0:T(8,128)(2,1)} %copy-done.1, ...), custom_call_target="tpu_custom_call" | custom-call | flops 2097152 | bytes 21758016 | tf_op jit(solution)/shard_map/pallas_call | solution.py:36
  23.2 0.0 collective-permute-done.1.refs_1_
  23.2 0.0 copy-start
  23.2 1.9 %shard_map.96.base = f32[4,256,256]{2,1,0:T(8,128)S(1)} custom-call(s32[2,4]{1,0:T(2,128)S(1)} %get-tuple-element.18.orbs, f32[1,4]{1,0:T(1,128)S(1)} %get-tuple-element.19.occ, s32[1,1]{1,0:T(1,128)S(6)} %copy.11.count, f32[4,256]{1,0:T(4,128)S(1)} %get-tuple-element.20.energy, bf16[4,256,256]{2,1,0:T(8,128)(2,1)} %amps.3, ...), custom_call_target="tpu_custom_call" | custom-call | flops 268435456 | bytes 25232192 | tf_op jit(solution)/shard_map/pallas_call | solution.py:36
  25.1 0.0 collective-permute-done.9.refs_1_
  25.1 0.0 collective-permute-done.8.refs_0_
  25.1 0.0 copy-done
  25.1 1.3 %shard_map.99 = f32[4,256,256]{2,1,0:T(8,128)} custom-call(s32[1,1]{1,0:T(1,128)S(6)} %copy.11.count, s32[4,4]{1,0:T(4,128)S(1)} %shard_map.95.token, f32[48,256]{1,0:T(8,128)S(1)} %reshape.5.weights, f32[4,256,256]{2,1,0:T(8,128)S(1)} %shard_map.96.base, bf16[4,256,256]{2,1,0:T(8,128)(2,1)S(1)} %copy-done, f32[4,256,256]{2,1,0:T(8,128)S(1)} %shard_map.98.sums, ...), custom_call_target="tpu_custom_call" | custom-call | flops 268435456 | bytes 46924864 | tf_op jit(solution)/shard_map/pallas_call | solution.py:36
  (9 shorter events, 0.1 us)
Async XLA Ops:
  0.0 9.9 %collective-permute-start = (bf16[4,128,256]{2,1,0:T(8,128)(2,1)}, bf16[4,128,256]{2,1,0:T(8,128)(2,1)S(1)}, u32[]{:S(2)}, u32[]{:S(2)}) collective-permute-start(bf16[4,128,256]{2,1,0:T(8,128)(2,1)} %param.9), channel_id=1, source_target_pairs={{0,16},{8,24},{16,0},{24,8},{1,17},{9,25},{17,1},{25,9},{2,18},{10... | collective-permute-start | bytes 786440 | tf_op jit(solution)/shard_map/ppermute | solution.py:211
  4.4 2.7 %copy-start.2 = (bf16[256,256]{1,0:T(8,128)(2,1)}, bf16[256,256]{1,0:T(8,128)(2,1)S(1)}, u32[]{:S(2)}) copy-start(bf16[256,256]{1,0:T(8,128)(2,1)S(1)} %get-tuple-element.21.refs_0_) | copy-start | bytes 393220
  4.4 5.6 %collective-permute-start.2 = (bf16[256,256]{1,0:T(8,128)(2,1)S(1)}, bf16[256,256]{1,0:T(8,128)(2,1)S(1)}, u32[]{:S(2)}, u32[]{:S(2)}) collective-permute-start(bf16[256,256]{1,0:T(8,128)(2,1)S(1)} %get-tuple-element.21.refs_0_), channel_id=1, source_target_pairs={{0,1},{1,0},{2,3},{3,2},{4,5},{5,4},{6,7},{7,6},{8,9},{9,8},{10,11... | collective-permute-start | bytes 393224 | tf_op jit(solution)/shard_map/ppermute | solution.py:279
  6.7 3.1 %copy-start.5 = (bf16[4,128,256]{2,1,0:T(8,128)(2,1)S(1)}, bf16[4,128,256]{2,1,0:T(8,128)(2,1)}, u32[]{:S(2)}) copy-start(bf16[4,128,256]{2,1,0:T(8,128)(2,1)} %param.9) | copy-start | bytes 786436
  7.2 2.7 %copy-start.3 = (bf16[256,256]{1,0:T(8,128)(2,1)}, bf16[256,256]{1,0:T(8,128)(2,1)S(1)}, u32[]{:S(2)}) copy-start(bf16[256,256]{1,0:T(8,128)(2,1)S(1)} %get-tuple-element.24.refs_1_) | copy-start | bytes 393220
  7.2 2.7 %copy-start.4 = (bf16[256,256]{1,0:T(8,128)(2,1)}, bf16[256,256]{1,0:T(8,128)(2,1)S(1)}, u32[]{:S(2)}) copy-start(bf16[256,256]{1,0:T(8,128)(2,1)S(1)} %get-tuple-element.25.refs_2_) | copy-start | bytes 393220
  7.2 9.3 %copy-start.1 = (bf16[256,256]{1,0:T(8,128)(2,1)}, bf16[256,256]{1,0:T(8,128)(2,1)S(1)}, u32[]{:S(2)}) copy-start(bf16[256,256]{1,0:T(8,128)(2,1)S(1)} %get-tuple-element.26.refs_3_) | copy-start | bytes 393220
  7.2 6.4 %collective-permute-start.3 = (bf16[256,256]{1,0:T(8,128)(2,1)S(1)}, bf16[256,256]{1,0:T(8,128)(2,1)S(1)}, u32[]{:S(2)}, u32[]{:S(2)}) collective-permute-start(bf16[256,256]{1,0:T(8,128)(2,1)S(1)} %get-tuple-element.24.refs_1_), channel_id=1, source_target_pairs={{0,1},{1,0},{2,3},{3,2},{4,5},{5,4},{6,7},{7,6},{8,9},{9,8},{10,11... | collective-permute-start | bytes 393224 | tf_op jit(solution)/shard_map/ppermute | solution.py:279
  7.8 8.7 %collective-permute-start.4 = (bf16[256,256]{1,0:T(8,128)(2,1)S(1)}, bf16[256,256]{1,0:T(8,128)(2,1)S(1)}, u32[]{:S(2)}, u32[]{:S(2)}) collective-permute-start(bf16[256,256]{1,0:T(8,128)(2,1)S(1)} %get-tuple-element.25.refs_2_), channel_id=1, source_target_pairs={{0,1},{1,0},{2,3},{3,2},{4,5},{5,4},{6,7},{7,6},{8,9},{9,8},{10,11... | collective-permute-start | bytes 393224 | tf_op jit(solution)/shard_map/ppermute | solution.py:279
  9.3 8.6 %collective-permute-start.5 = (bf16[256,256]{1,0:T(8,128)(2,1)S(1)}, bf16[256,256]{1,0:T(8,128)(2,1)S(1)}, u32[]{:S(2)}, u32[]{:S(2)}) collective-permute-start(bf16[256,256]{1,0:T(8,128)(2,1)S(1)} %get-tuple-element.26.refs_3_), channel_id=1, source_target_pairs={{0,1},{1,0},{2,3},{3,2},{4,5},{5,4},{6,7},{7,6},{8,9},{9,8},{10,11... | collective-permute-start | bytes 393224 | tf_op jit(solution)/shard_map/ppermute | solution.py:279
  9.9 13.3 %collective-permute-start.1 = (bf16[4,256,256]{2,1,0:T(8,128)(2,1)S(1)}, bf16[4,256,256]{2,1,0:T(8,128)(2,1)S(1)}, u32[]{:S(2)}, u32[]{:S(2)}) collective-permute-start(bf16[4,256,256]{2,1,0:T(8,128)(2,1)S(1)} %constant_dynamic-update-slice_fusion.refs_0_), channel_id=1, source_target_pairs={{0,8},{8,0},{16,24},{24,16},{1,9},{9,1},{17,25},{25,17},{2,10},{10... | collective-permute-start | bytes 1572872 | tf_op jit(solution)/shard_map/ppermute | solution.py:211
  10.0 10.5 %collective-permute-start.6 = (bf16[256,256]{1,0:T(8,128)(2,1)S(1)}, bf16[256,256]{1,0:T(8,128)(2,1)S(1)}, u32[]{:S(2)}, u32[]{:S(2)}) collective-permute-start(bf16[256,256]{1,0:T(8,128)(2,1)S(1)} %collective-permute-done.2.refs_4_), channel_id=1, source_target_pairs={{0,2},{1,7},{2,4},{3,1},{4,6},{5,3},{6,0},{7,5},{8,10},{9,15},{10,... | collective-permute-start | bytes 393224 | tf_op jit(solution)/shard_map/ppermute | solution.py:280
  13.6 8.1 %collective-permute-start.7 = (bf16[256,256]{1,0:T(8,128)(2,1)S(1)}, bf16[256,256]{1,0:T(8,128)(2,1)S(1)}, u32[]{:S(2)}, u32[]{:S(2)}) collective-permute-start(bf16[256,256]{1,0:T(8,128)(2,1)S(1)} %collective-permute-done.3.refs_5_), channel_id=1, source_target_pairs={{0,2},{1,7},{2,4},{3,1},{4,6},{5,3},{6,0},{7,5},{8,10},{9,15},{10,... | collective-permute-start | bytes 393224 | tf_op jit(solution)/shard_map/ppermute | solution.py:280
  16.5 8.7 %collective-permute-start.9 = (bf16[256,256]{1,0:T(8,128)(2,1)S(1)}, bf16[256,256]{1,0:T(8,128)(2,1)S(1)}, u32[]{:S(2)}, u32[]{:S(2)}) collective-permute-start(bf16[256,256]{1,0:T(8,128)(2,1)S(1)} %get-tuple-element.26.refs_3_), channel_id=1, source_target_pairs={{1,2},{2,1},{3,4},{4,3},{5,6},{6,5},{0,8},{7,15},{9,10},{10,9},{11... | collective-permute-start | bytes 393224 | tf_op jit(solution)/shard_map/ppermute | solution.py:281
  17.9 7.2 %collective-permute-start.8 = (bf16[256,256]{1,0:T(8,128)(2,1)S(1)}, bf16[256,256]{1,0:T(8,128)(2,1)S(1)}, u32[]{:S(2)}, u32[]{:S(2)}) collective-permute-start(bf16[256,256]{1,0:T(8,128)(2,1)S(1)} %collective-permute-done.4.refs_6_), channel_id=1, source_target_pairs={{0,2},{2,4},{4,6},{6,7},{7,5},{5,3},{3,1},{1,0},{8,10},{10,12},{12... | collective-permute-start | bytes 393224 | tf_op jit(solution)/shard_map/ppermute | solution.py:280
  23.2 1.9 %copy-start = (bf16[4,256,256]{2,1,0:T(8,128)(2,1)S(1)}, bf16[4,256,256]{2,1,0:T(8,128)(2,1)}, u32[]{:S(2)}) copy-start(bf16[4,256,256]{2,1,0:T(8,128)(2,1)} %bases.3) | copy-start | bytes 1572868
